TPU v7x, 32 devices: a whole 2x2x4 slice. The times are simulated.
32 devices in a mesh: seq: 4 (over y, x), grp: 8 (over z, core).
Axes of the slice: x: 2, y: 2, z: 4, core: 2. Of those that a mesh axis runs over, the one named last changes fastest.
Arguments:
- tokens: bfloat16 [16384, 768], P(('grp', 'seq')), may hold values from -6 to 6
- cotangent: bfloat16 [16384, 768], P(('grp', 'seq')), may hold values from -6 to 6
- seq_len: int32 [8], P('grp'), may hold values from 1024 to 2048, as said below
- weight_mats: bfloat16 [768, 9280], replicated
- weight_vecs: bfloat16 [768, 13], replicated
- master_mats: float32 [768, 9280], P('grp'), may hold values from -0.21875 to 0.21875
- master_vecs: float32 [768, 13], P('grp'), may hold values from -3 to 3
- moment_mats: float32 [768, 9280], P('grp'), may hold values from -384 to 384
- moment_vecs: float32 [768, 13], P('grp'), may hold values from -384 to 384
- square_mats: float32 [768, 9280], P('grp'), may hold values from 819.2 to 32768
- square_vecs: float32 [768, 13], P('grp'), may hold values from 819.2 to 32768
- average_mats: float32 [768, 9280], P('grp'), may hold values from -0.21875 to 0.21875
- average_vecs: float32 [768, 13], P('grp'), may hold values from -3 to 3
Outputs:
- block_output: bfloat16 [16384, 768], P(('grp', 'seq'))
- input_grad: bfloat16 [16384, 768], P(('grp', 'seq'))
- grad_mats: float32 [768, 9280], P('grp')
- grad_vecs: float32 [768, 13], P('grp')
- master_mats_new: float32 [768, 9280], P('grp')
- master_vecs_new: float32 [768, 13], P('grp')
- moment_mats_new: float32 [768, 9280], P('grp')
- moment_vecs_new: float32 [768, 13], P('grp')
- square_mats_new: float32 [768, 9280], P('grp')
- square_vecs_new: float32 [768, 13], P('grp')
- average_mats_new: float32 [768, 9280], P('grp')
- average_vecs_new: float32 [768, 13], P('grp')
- copy_mats: bfloat16 [768, 9280], P('grp')
- copy_vecs: bfloat16 [768, 13], P('grp')
Inputs may be any that keep to these rules, and one draw needn't show every extreme that they name: Each group's sequences all have the length seq_len of that group; both values 2 * 512 and 2048 occur in every draw.
All inputs are finite; a program needn't handle non-finite values.
Results may differ from a plain program's by a relative error of at most 0.018.
Values may be sent and summed in bfloat16 or wider, within the bound.
No kernel may reach another device: no remote copies, remote signals or barrier semaphores. Data moves between devices by JAX's collectives and lax.ppermute only.
A program may use at most 192 MiB of HBM per device.

v0:
```python
from functools import partial
import jax
import jax.numpy as jnp
from jax import lax
from jax.sharding import PartitionSpec as P

D = 768
HEADS = 12
HD = 64
FF = 3072
norm_eps = 1e-05
adam_eps = 1e-08
beta_first = 0.5
beta_second = 0.5
learn_rate = 0.01
vector_rate = 0.06
decay_rate = 0.1
average_keep = 0.9
highest = lax.Precision.HIGHEST
careful_level = lax.Precision.HIGH


def contract_rows(left, right):
    return lax.dot_general(
        left, right, (((0,), (0,)), ((), ())), preferred_element_type=jnp.float32
    )


def contract_cols(left, right):
    return lax.dot_general(
        left, right, (((1,), (1,)), ((), ())), preferred_element_type=jnp.float32
    )


def precise(left, right):
    return jnp.dot(left, right, preferred_element_type=jnp.float32, precision=careful_level)


def norm_rows(values, gain, shift):
    average = jnp.mean(values, axis=1, keepdims=True)
    centered = values - average
    variance = jnp.mean(centered * centered, axis=1, keepdims=True)
    return centered * lax.rsqrt(variance + norm_eps) * gain + shift


def norm_back(values, gain, upstream):
    average = jnp.mean(values, axis=1, keepdims=True)
    centered = values - average
    variance = jnp.mean(centered * centered, axis=1, keepdims=True)
    inverse = lax.rsqrt(variance + norm_eps)
    normed = centered * inverse
    d_gain = jnp.sum(upstream * normed, axis=0)
    d_shift = jnp.sum(upstream, axis=0)
    d_normed = upstream * gain
    d_values = inverse * (
        d_normed
        - jnp.mean(d_normed, axis=1, keepdims=True)
        - normed * jnp.mean(d_normed * normed, axis=1, keepdims=True)
    )
    return (d_values, d_gain, d_shift)


def feature_map(values, hedge_map):
    count = values.shape[0]
    per_head = values.reshape(count, HEADS, HD)
    scores = jnp.einsum("nhi,hij->nhj", per_head, hedge_map, precision=highest)
    return jnp.concatenate(
        [jax.nn.softmax(scores, axis=-1), jax.nn.softmax(-scores, axis=-1)], axis=-1
    )


def adam_step(grad, master, first, second, rate):
    new_first = beta_first * first + (1.0 - beta_first) * grad
    new_second = beta_second * second + (1.0 - beta_second) * grad * grad
    new_master = master - rate * (
        new_first / (jnp.sqrt(new_second) + adam_eps) + decay_rate * master
    )
    return (new_master, new_first, new_second)


def on_device(
    tokens,
    cotangent,
    seq_len,
    weight_mats,
    weight_vecs,
    master_mats,
    master_vecs,
    moment_mats,
    moment_vecs,
    square_mats,
    square_vecs,
    average_mats,
    average_vecs,
):
    rows = tokens.shape[0]
    my_start = lax.axis_index("seq") * rows
    seq_length = seq_len[0]
    starts = (my_start % seq_length == 0).astype(jnp.float32)
    continued = 1.0 - starts
    w_qkv = weight_mats[:, : 3 * D]
    w_proj = weight_mats[:, 3 * D : 4 * D]
    w_fc = weight_mats[:, 4 * D : 4 * D + FF]
    w_down = weight_mats[:, 4 * D + FF : 4 * D + 2 * FF]
    hedge_map = weight_mats[:, 4 * D + 2 * FF :].astype(jnp.float32).reshape(HEADS, HD, HD)
    vec_all = weight_vecs.astype(jnp.float32)
    gain_one = vec_all[:, 0]
    gain_two = vec_all[:, 2]
    bias_qkv = vec_all[:, 6:9].T.reshape(3 * D)
    bias_fc = vec_all[:, 9:].T.reshape(FF)
    line_index = jnp.arange(rows, dtype=jnp.int32)
    causal = (line_index[:, None] >= line_index[None, :]).astype(jnp.float32)
    inputs = tokens.astype(jnp.float32)
    normed_low = norm_rows(inputs, gain_one, vec_all[:, 1]).astype(jnp.bfloat16)
    projected = jnp.dot(normed_low, w_qkv, preferred_element_type=jnp.float32) + bias_qkv
    queries = projected[:, :D]
    keys = projected[:, D : 2 * D]
    values_low = projected[:, 2 * D :].astype(jnp.bfloat16)
    query_full, query_back = jax.vjp(feature_map, queries, hedge_map)
    key_full, key_back = jax.vjp(feature_map, keys, hedge_map)
    query_feat = query_full.astype(jnp.bfloat16)
    key_feat = key_full.astype(jnp.bfloat16)
    value_heads = values_low.reshape(rows, HEADS, HD)
    gath_keys, gath_values = (
        lax.all_gather(key_feat.reshape(rows, 2 * D), "seq", axis=0, tiled=True),
        lax.all_gather(values_low, "seq", axis=0, tiled=True),
    )
    positions = jnp.arange(gath_keys.shape[0], dtype=jnp.int32)
    keep_rows = (
        (positions < my_start) & (positions // seq_length == my_start // seq_length)
    ).astype(jnp.bfloat16)
    kept_keys = (gath_keys * keep_rows[:, None]).reshape(-1, HEADS, 2 * HD)
    state_in = jnp.einsum(
        "nhf,nhd->hfd",
        kept_keys,
        gath_values.reshape(-1, HEADS, HD),
        preferred_element_type=jnp.float32,
    )
    total_in = jnp.sum(kept_keys, axis=0, dtype=jnp.float32)
    query_heads = jnp.transpose(query_feat, (1, 0, 2))
    key_heads = jnp.transpose(key_feat, (1, 0, 2))
    value_major = jnp.transpose(value_heads, (1, 0, 2))

    def attend(parts):
        query_part, key_part, value_part, state, total = parts
        query_wide = query_part.astype(jnp.float32)
        weights = jnp.dot(query_part, key_part.T, preferred_element_type=jnp.float32) * causal
        numer = precise(weights, value_part.astype(jnp.float32)) + precise(query_wide, state)
        denom = jnp.sum(weights, axis=1) + precise(query_wide, total)
        return (numer / denom[:, None], denom)

    head_outs, denoms = lax.map(attend, (query_heads, key_heads, value_major, state_in, total_in))
    mixed_low = jnp.transpose(head_outs, (1, 0, 2)).reshape(rows, D).astype(jnp.bfloat16)
    attn_out = jnp.dot(mixed_low, w_proj, preferred_element_type=jnp.float32) + vec_all[:, 4]
    resid = inputs + attn_out
    normed_two_low = norm_rows(resid, gain_two, vec_all[:, 3]).astype(jnp.bfloat16)
    hidden_pre = jnp.dot(normed_two_low, w_fc, preferred_element_type=jnp.float32) + bias_fc
    hidden_act, gelu_back = jax.vjp(partial(jax.nn.gelu, approximate=True), hidden_pre)
    hidden_low = hidden_act.astype(jnp.bfloat16)
    result = resid + contract_cols(hidden_low, w_down) + vec_all[:, 5]
    block_output = result.astype(jnp.bfloat16)
    grad_out = cotangent.astype(jnp.float32)
    d_down = contract_rows(cotangent, hidden_low)
    d_bias_down = jnp.sum(grad_out, axis=0)
    d_hidden = jnp.dot(cotangent, w_down, preferred_element_type=jnp.float32)
    d_pre_low = gelu_back(d_hidden)[0].astype(jnp.bfloat16)
    d_fc = contract_rows(normed_two_low, d_pre_low)
    d_bias_fc = jnp.sum(d_pre_low.astype(jnp.float32), axis=0)
    d_normed_two = contract_cols(d_pre_low, w_fc)
    d_resid_norm, d_gain_two, d_shift_two = norm_back(resid, gain_two, d_normed_two)
    d_resid = grad_out + d_resid_norm
    d_attn_low = d_resid.astype(jnp.bfloat16)
    d_bias_proj = jnp.sum(d_attn_low.astype(jnp.float32), axis=0)
    d_proj = contract_rows(mixed_low, d_attn_low)
    d_mixed_low = lax.optimization_barrier(contract_cols(d_attn_low, w_proj).astype(jnp.bfloat16))
    d_mixed = jnp.transpose(d_mixed_low.astype(jnp.float32).reshape(rows, HEADS, HD), (1, 0, 2))

    def attend_back(parts):
        query_part, key_part, value_part, state, total, outs, denom, upstream = parts
        query_wide = query_part.astype(jnp.float32)
        key_wide = key_part.astype(jnp.float32)
        weights = jnp.dot(query_part, key_part.T, preferred_element_type=jnp.float32) * causal
        ratio = upstream / denom[:, None]
        offset = -jnp.sum(upstream * outs, axis=1) / denom
        d_weights = (precise(ratio, value_part.astype(jnp.float32).T) + offset[:, None]) * causal
        d_query = (
            precise(d_weights, key_wide)
            + precise(ratio, state.T)
            + offset[:, None] * total[None, :]
        )
        d_key = precise(d_weights.T, query_wide)
        d_value = precise(weights.T, ratio)
        back_state = precise(query_wide.T, ratio) * continued
        back_total = precise(offset, query_wide) * continued
        return (d_query, d_key, d_value, back_state, back_total)

    d_query_h, d_key_h, d_value_h, back_state, back_total = lax.map(
        attend_back,
        (query_heads, key_heads, value_major, state_in, total_in, head_outs, denoms, d_mixed),
    )
    count = rows * lax.axis_size("seq")
    keys_part = gath_keys.astype(jnp.float32).reshape(count, HEADS, 2 * HD)
    vals_part = gath_values.astype(jnp.float32).reshape(count, HEADS, HD)
    keep_part = keep_rows.astype(jnp.float32)
    d_keys_part = (
        jnp.einsum("nhd,hfd->nhf", vals_part, back_state, precision=careful_level)
        + back_total[None]
    ) * keep_part[:, None, None]
    d_vals_part = (
        jnp.einsum("nhf,hfd->nhd", keys_part, back_state, precision=careful_level)
        * keep_part[:, None, None]
    )
    remote = lax.psum_scatter(
        jnp.concatenate(
            [d_keys_part.reshape(count, 2 * D), d_vals_part.reshape(count, D)], axis=1
        ).astype(jnp.bfloat16),
        "seq",
        scatter_dimension=0,
        tiled=True,
    ).astype(jnp.float32)
    d_key_extra = remote[:, : 2 * D].reshape(rows, HEADS, 2 * HD)
    d_value_extra = remote[:, 2 * D :].reshape(rows, HEADS, HD)
    d_query_all = jnp.transpose(d_query_h, (1, 0, 2))
    d_key_all = jnp.transpose(d_key_h, (1, 0, 2)) + d_key_extra
    d_value_all = jnp.transpose(d_value_h, (1, 0, 2)) + d_value_extra
    d_queries, d_map_query = query_back(d_query_all)
    d_keys, d_map_key = key_back(d_key_all)
    d_proj_low = jnp.concatenate([d_queries, d_keys, d_value_all.reshape(rows, D)], axis=1).astype(
        jnp.bfloat16
    )
    d_qkv = contract_rows(normed_low, d_proj_low)
    d_bias_qkv = jnp.sum(d_proj_low.astype(jnp.float32), axis=0)
    d_normed_one = contract_cols(d_proj_low, w_qkv)
    d_input_norm, d_gain_one, d_shift_one = norm_back(inputs, gain_one, d_normed_one)
    input_grad = (d_resid + d_input_norm).astype(jnp.bfloat16)
    grad_mats = jnp.concatenate(
        [d_qkv, d_proj, d_fc, d_down, (d_map_query + d_map_key).reshape(D, HD)], axis=1
    )
    grad_vecs = jnp.concatenate(
        [
            jnp.stack(
                [d_gain_one, d_shift_one, d_gain_two, d_shift_two, d_bias_proj, d_bias_down], axis=1
            ),
            d_bias_qkv.reshape(3, D).T,
            d_bias_fc.reshape(FF // D, D).T,
        ],
        axis=1,
    )
    owned_mats, owned_vecs = (
        lax.psum_scatter(grad_mats, "grp", scatter_dimension=0, tiled=True),
        lax.psum_scatter(grad_vecs, "grp", scatter_dimension=0, tiled=True),
    )
    grad_mats_own, grad_vecs_own = (
        lax.psum(owned_mats.astype(jnp.bfloat16), "seq").astype(jnp.float32),
        lax.psum(owned_vecs.astype(jnp.bfloat16), "seq").astype(jnp.float32),
    )
    new_mats, new_first_m, new_second_m = adam_step(
        grad_mats_own, master_mats, moment_mats, square_mats, learn_rate
    )
    new_vecs, new_first_v, new_second_v = adam_step(
        grad_vecs_own, master_vecs, moment_vecs, square_vecs, vector_rate
    )
    new_avg_m = average_keep * average_mats + (1.0 - average_keep) * new_mats
    new_avg_v = average_keep * average_vecs + (1.0 - average_keep) * new_vecs
    return (
        block_output,
        input_grad,
        grad_mats_own,
        grad_vecs_own,
        new_mats,
        new_vecs,
        new_first_m,
        new_first_v,
        new_second_m,
        new_second_v,
        new_avg_m,
        new_avg_v,
        new_mats.astype(jnp.bfloat16),
        new_vecs.astype(jnp.bfloat16),
    )


def solution(mesh):
    in_specs = (
        P(("grp", "seq"), None),
        P(("grp", "seq"), None),
        P("grp"),
        P(),
        P(),
        P("grp", None),
        P("grp", None),
        P("grp", None),
        P("grp", None),
        P("grp", None),
        P("grp", None),
        P("grp", None),
        P("grp", None),
    )
    out_specs = (
        P(("grp", "seq"), None),
        P(("grp", "seq"), None),
        P("grp", None),
        P("grp", None),
        P("grp", None),
        P("grp", None),
        P("grp", None),
        P("grp", None),
        P("grp", None),
        P("grp", None),
        P("grp", None),
        P("grp", None),
        P("grp", None),
        P("grp", None),
    )
    return jax.shard_map(
        on_device, mesh=mesh, in_specs=in_specs, out_specs=out_specs, check_vma=False
    )
```

profile of v0, /device:TPU:0, one launch (start us, length us, event | category | flops | bytes accessed | tf_op | source)
XLA Modules:
  0.0 1010.2 jit_solution(10283826518961896790)
XLA Ops:
  11.6 4.2 convolution_add_fusion.3
  19.1 3.3 fusion.162
  25.0 2.4 fusion.165
  45.7 3.1 copy.80
  50.2 2.6 copy.81
  53.0 12.7 %all-gather.5.cloned.1.call-done = bf16[2048,768]{1,0:T(8,128)(2,1)} async-done(((bf16[512,768]{1,0:T(8,128)(2,1)}), bf16[2048,768]{1,0:T(8,128)(2,1)}) %all-gather.5.cloned.1.call-update) | async-done | bytes 3145744 | tf_op jit(solution)/shard_map/all_gather | solution.py:126
  65.8 4.6 copy.78
  70.4 67.8 %all-gather.3.cloned.1.call-done = bf16[2048,1536]{0,1:T(8,128)(2,1)} async-done(((bf16[512,1536]{0,1:T(8,128)(2,1)}), bf16[2048,1536]{0,1:T(8,128)(2,1)}) %all-gather.3.cloned.1.call-update) | async-done | bytes 6291472 | tf_op jit(solution)/shard_map/all_gather | solution.py:125
  138.2 5.0 convert_reduce_fusion
  146.4 81.3 %while.33 = (s32[]{:T(128)}, f32[12,512,64]{1,2,0:T(8,128)}, f32[12,512]{1,0:T(8,128)}, bf16[12,512,128]{2,1,0:T(8,128)(2,1)}, bf16[12,512,128]{2,1,0:T(8,128)(2...) while((s32[]{:T(128)}, f32[12,512,64]{1,2,0:T(8,128)}, ...), condition=%wide.region_13.14_spmd.clone, body=%wide.region_11.13_spmd.clone.sunk | while | flops 194183168 | bytes 3231861 | solution.py:152
  229.5 2.4 fusion.167
  232.4 5.0 fusion.85
  237.4 11.5 %convert_reduce_fusion.1 = (f32[3072]{0:T(1024)}, bf16[512,3072]{1,0:T(8,128)(2,1)S(1)}) fusion(f32[512,3072]{1,0:T(8,128)S(1)} %fusion.85, f32[3072]{0:T(1024)S(1)} %add.216, bf16[512,768]{1,0:T(8,128)(2,1)S(1)} %copy-done.40, bf16[768,9280]{0,1:T(8,128)(2,1)} %param.20), kind=kOutput, calls=%fused_computation.105 | convolution fusion | flops 2452091904 | bytes 14966784 | tf_op jit(solution)/shard_map/dot_general | solution.py:165
  249.0 3.5 multiply_reduce_fusion
  258.5 202.7 %while.34 = (s32[]{:T(128)}, f32[12,512,128]{1,2,0:T(8,128)}, f32[12,512,128]{1,2,0:T(8,128)}, f32[12,512,64]{1,2,0:T(8,128)}, f32[12,128,64]{1,2,0:T(8,128)}, /...) while((s32[]{:T(128)}, f32[12,512,128]{1,2,0:T(8,128)}, ...), condition=%wide.region_20.21_spmd.clone.clone, body=%wide.region_18.20_spmd.clone.clone.sunk | while | flops 723526784 | bytes 10363109 | solution.py:197
  461.3 5.1 multiply_convert_fusion.1
  466.4 5.4 multiply_convert_fusion
  471.8 11.6 %pad_maximum_fusion = bf16[2048,2304]{0,1:T(8,128)(2,1)} fusion(bf16[2048,768]{0,1:T(8,128)(2,1)S(1)} %bitcast.307, bf16[2048,1536]{0,1:T(8,128)(2,1)S(1)} %bitcast.302), kind=kLoop, calls=%fused_computation.92 | loop fusion | flops 18874368 | bytes 18874368 | tf_op jit(solution)/shard_map/concatenate | solution.py:214
  484.8 3.4 multiply_reduce_fusion.4
  491.5 87.1 %reduce-scatter.6.cloned.1.call-done = bf16[512,2304]{0,1:T(8,128)(2,1)} async-done(((bf16[2048,2304]{0,1:T(8,128)(2,1)}), bf16[512,2304]{0,1:T(8,128)(2,1)}) %reduce-scatter.6.cloned.1.call-update) | async-done | bytes 2359312 | tf_op jit(solution)/shard_map/reduce_scatter | solution.py:213
  592.2 5.4 convolution_dynamic-update-slice_fusion
  600.0 5.5 convolution_dynamic-update-slice_fusion.1
  605.5 5.5 bitcast_dynamic-update-slice_fusion
  614.4 6.0 fusion.110
  621.8 270.7 %reduce-scatter.8.cloned.1.call-done = f32[96,9280]{1,0:T(8,128)} async-done(((f32[768,9280]{1,0:T(8,128)}), f32[96,9280]{1,0:T(8,128)}) %reduce-scatter.8.cloned.1.call-update) | async-done | bytes 3563536 | tf_op jit(solution)/shard_map/reduce_scatter | solution.py:250
  892.5 3.4 convert_element_type.146
  896.6 9.6 add_convert_fusion
  907.7 16.4 %reduce-scatter.10.cloned.1.call-done = f32[96,13]{1,0:T(8,128)} async-done(((f32[768,13]{1,0:T(8,128)}), f32[96,13]{1,0:T(8,128)}) %reduce-scatter.10.cloned.1.call-update) | async-done | bytes 5008
  925.0 10.0 psum.15
  936.3 54.8 %all-reduce.2.cloned.1.call-done = bf16[96,9280]{1,0:T(8,128)(2,1)} async-done(((bf16[96,9280]{1,0:T(8,128)(2,1)}), bf16[96,9280]{1,0:T(8,128)(2,1)}) %all-reduce.2.cloned.1.call-update) | async-done | bytes 1781776 | tf_op jit(solution)/shard_map/psum | solution.py:254
  991.1 8.9 fusion.158
  1000.1 2.8 multiply_add_fusion.1
  (577 shorter events, 353.1 us)
Async XLA Ops:
  7.2 58.6 %all-gather.5.cloned.1.call-start = ((), (), s32[]{:S(2)}) async-start(), calls=%async_computation.4 | async-start | bytes 3932160 | tf_op jit(solution)/shard_map/all_gather | solution.py:126
  8.7 7.1 copy-start.53
  8.7 7.1 copy-start.71
  8.7 223.7 %copy-start.69 = (f32[768]{0:T(1024)}, f32[768]{0:T(1024)S(1)}, u32[]{:S(2)}) copy-start(f32[768]{0:T(1024)S(1)} %get-tuple-element.327) | copy-start | bytes 9220
  8.7 243.8 %copy-start.51 = (f32[768]{0:T(1024)}, f32[768]{0:T(1024)S(1)}, u32[]{:S(2)}) copy-start(f32[768]{0:T(1024)S(1)} %get-tuple-element.325) | copy-start | bytes 9220
  10.0 5.7 copy-start.45
  18.9 119.3 %all-gather.3.cloned.1.call-start = ((), (), s32[]{:S(2)}) async-start(), calls=%async_computation.3 | async-start | bytes 7864320 | tf_op jit(solution)/shard_map/all_gather | solution.py:125
  19.1 18.3 %copy-start.30 = (bf16[768,64]{1,0:T(8,128)(2,1)}, bf16[768,64]{1,0:T(8,128)(2,1)S(1)}, u32[]{:S(2)}) copy-start(bf16[768,64]{1,0:T(8,128)(2,1)S(1)} %copy.136) | copy-start | bytes 294916
  32.5 546.0 %reduce-scatter.6.cloned.1.call-start = ((), (), s32[]{:S(2)}) async-start(), calls=%async_computation.5 | async-start | bytes 11796480 | tf_op jit(solution)/shard_map/reduce_scatter | solution.py:213
  34.0 203.4 %copy-start.55 = (f32[3072]{0:T(1024)}, f32[3072]{0:T(1024)S(1)}, u32[]{:S(2)}) copy-start(f32[3072]{0:T(1024)S(1)} %add.216) | copy-start | bytes 36868
  232.0 20.5 %copy-start.27 = (f32[512,768]{1,0:T(8,128)}, f32[512,768]{1,0:T(8,128)S(1)}, u32[]{:S(2)}) copy-start(f32[512,768]{1,0:T(8,128)S(1)} %get-tuple-element.409) | copy-start | bytes 4718596
  232.0 20.5 %copy-start.47 = (f32[512]{0:T(512)}, f32[512]{0:T(512)S(1)}, u32[]{:S(2)}) copy-start(f32[512]{0:T(512)S(1)} %broadcast_multiply_fusion.5) | copy-start | bytes 6148
  232.3 20.2 %copy-start.60 = (f32[512]{0:T(512)}, f32[512]{0:T(512)S(1)}, u32[]{:S(2)}) copy-start(f32[512]{0:T(512)S(1)} %add_rsqrt_fusion) | copy-start | bytes 6148
  232.4 16.6 %slice-start = ((s8[14254080]{0:T(1024)(128)(4,1)}), s8[4194304]{0:T(1024)(128)(4,1)S(1)}, s32[]{:S(2)}) async-start(s8[14254080]{0:T(1024)(128)(4,1)} %bitcast.338), calls=%async_computation.9 | async-start | bytes 8388608
  232.4 16.6 %slice-start.1 = ((s8[14254080]{0:T(1024)(128)(4,1)}), s8[4194304]{0:T(1024)(128)(4,1)S(1)}, s32[]{:S(2)}) async-start(s8[14254080]{0:T(1024)(128)(4,1)} %bitcast.338), calls=%async_computation.10 | async-start | bytes 8388608
  237.4 11.5 %copy-start.78 = (f32[512,3072]{1,0:T(8,128)}, f32[512,3072]{1,0:T(8,128)S(1)}, u32[]{:S(2)}) copy-start(f32[512,3072]{1,0:T(8,128)S(1)} %fusion.85) | copy-start | bytes 18874372
  237.4 11.5 %slice-start.2 = ((s8[14254080]{0:T(1024)(128)(4,1)}), s8[4194304]{0:T(1024)(128)(4,1)S(1)}, s32[]{:S(2)}) async-start(s8[14254080]{0:T(1024)(128)(4,1)} %bitcast.338), calls=%async_computation.11 | async-start | bytes 8388608
  237.4 11.5 %slice-start.3 = ((s8[14254080]{0:T(1024)(128)(4,1)}), s8[1671168]{0:T(1024)(128)(4,1)S(1)}, s32[]{:S(2)}) async-start(s8[14254080]{0:T(1024)(128)(4,1)} %bitcast.338), calls=%async_computation.12 | async-start | bytes 3342336
  483.4 409.1 %reduce-scatter.8.cloned.1.call-start = ((), (), s32[]{:S(2)}) async-start(), calls=%async_computation.6 | async-start | bytes 32292864 | tf_op jit(solution)/shard_map/reduce_scatter | solution.py:250
  591.5 6.2 copy-start.38
  592.2 7.7 copy-start.77
  597.7 7.8 slice-start.5
  599.9 5.6 copy-start.41
  611.9 312.3 %reduce-scatter.10.cloned.1.call-start = ((), (), s32[]{:S(2)}) async-start(), calls=%async_computation.8 | async-start | bytes 442368
  621.5 369.6 %all-reduce.2.cloned.1.call-start = ((), (), s32[]{:S(2)}) async-start(), calls=%async_computation.7 | async-start | bytes 3588096 | tf_op jit(solution)/shard_map/psum | solution.py:254
  896.6 9.6 copy-start.39
  906.2 28.8 %copy-start.63 = (f32[96,13]{0,1:T(8,128)S(1)}, f32[96,13]{0,1:T(8,128)}, u32[]{:S(2)}) copy-start(f32[96,13]{0,1:T(8,128)} %param.23) | copy-start | bytes 14980
  906.2 28.8 %copy-start.64 = (f32[96,13]{0,1:T(8,128)S(1)}, f32[96,13]{0,1:T(8,128)}, u32[]{:S(2)}) copy-start(f32[96,13]{0,1:T(8,128)} %param.27) | copy-start | bytes 14980
  906.3 28.8 %copy-start.65 = (f32[96,13]{0,1:T(8,128)S(1)}, f32[96,13]{0,1:T(8,128)}, u32[]{:S(2)}) copy-start(f32[96,13]{0,1:T(8,128)} %param.25) | copy-start | bytes 14980
  906.3 29.4 %copy-start.62 = (f32[96,13]{0,1:T(8,128)S(1)}, f32[96,13]{0,1:T(8,128)}, u32[]{:S(2)}) copy-start(f32[96,13]{0,1:T(8,128)} %param.29) | copy-start | bytes 14980
  935.7 64.4 %copy-start.44 = (f32[96,13]{0,1:T(8,128)}, f32[96,13]{0,1:T(8,128)S(1)}, u32[]{:S(2)}) copy-start(f32[96,13]{0,1:T(8,128)S(1)} %get-tuple-element.378) | copy-start | bytes 14980
  991.1 8.9 copy-start.32
  (71 other events, 170.4 us)
Sparse Core Ops, SparseCore 0:
  19.0 46.6 all-gather.4
  68.2 70.0 all-gather.2
  483.5 95.0 reduce-scatter.5
  612.0 280.4 reduce-scatter.7
  895.2 28.9 reduce-scatter.9
  928.2 62.9 all-reduce.1
where the time goes:
time: 1020 us; the launch traced here: 1010 us
  waiting for transfers between devices  510 us (50%)
  matrix products  282 us (28%)
  local copies, waits for them, and re-layouts  123 us (12%)
  other arithmetic  67.8 us (7%)
  between operations  16.2 us (2%)
    reduce_scatter x1, waiting for transfers between devices, on_device(): lax.psum_scatter(grad_mats, 'grp', scatter_dimension=0, tiled=True)  271 us
    dot_general x120, matrix products, precise(): jnp.dot(left, right, preferred_element_type=jnp.float32, precision=carefu...  171 us
    reduce_scatter x1, waiting for transfers between devices, on_device(): lax.psum_scatter(jnp.concatenate([d_keys_part.reshape(count, 2 * D), d_va...  87.1 us
    all_gather x1, waiting for transfers between devices, on_device(): lax.all_gather(key_feat.reshape(rows, 2 * D), 'seq', axis=0, tiled=True)  67.8 us
    psum x1, waiting for transfers between devices, on_device(): lax.psum(owned_mats.astype(jnp.bfloat16), 'seq').astype(jnp.float32)  54.8 us
    dynamic_update_slice x36, local copies, waits for them, and re-layouts, on_device(): lax.map(attend_back, (query_heads, key_heads, value_major, state_in, tota...  25.7 us
    dynamic_slice x48, local copies, waits for them, and re-layouts, on_device(): lax.map(attend_back, (query_heads, key_heads, value_major, state_in, tota...  23.5 us
    unnamed x173, local copies, waits for them, and re-layouts  23.3 us
  transfers between devices with their start and end apart: 6, of which 6 were waited for; matrix products, arithmetic and copies ran while one was open for 7% of the time, Pallas kernels for 0%

commit v1 on v0

--- a/solution.py
+++ b/solution.py
@@ -18,6 +18,24 @@
 average_keep = 0.9
 highest = lax.Precision.HIGHEST
 careful_level = lax.Precision.HIGH
+
+
+def ring_gather(array, axis, dim):
+    ways, here, hop = (lax.axis_size(axis), lax.axis_index(axis), array.shape[dim])
+    lengths = [n * ways if d == dim else n for d, n in enumerate(array.shape)]
+    full = lax.dynamic_update_slice_in_dim(
+        jnp.zeros(lengths, array.dtype), array, here * hop, axis=dim
+    )
+    going_up = going_down = array
+    for far in range(1, ways // 2 + 1):
+        going_up = lax.ppermute(going_up, axis, [(d, (d + 1) % ways) for d in range(ways)])
+        full = lax.dynamic_update_slice_in_dim(full, going_up, (here - far) % ways * hop, axis=dim)
+        if 2 * far < ways:
+            going_down = lax.ppermute(going_down, axis, [(d, (d - 1) % ways) for d in range(ways)])
+            full = lax.dynamic_update_slice_in_dim(
+                full, going_down, (here + far) % ways * hop, axis=dim
+            )
+    return full
 
 
 def contract_rows(left, right):
@@ -122,7 +140,7 @@
     key_feat = key_full.astype(jnp.bfloat16)
     value_heads = values_low.reshape(rows, HEADS, HD)
     gath_keys, gath_values = (
-        lax.all_gather(key_feat.reshape(rows, 2 * D), "seq", axis=0, tiled=True),
+        ring_gather(key_feat.reshape(rows, 2 * D), "seq", 0),
         lax.all_gather(values_low, "seq", axis=0, tiled=True),
     )
     positions = jnp.arange(gath_keys.shape[0], dtype=jnp.int32)

time: 1020 us -> 1050 us (1.029)
  waiting for transfers between devices: 510 us -> 524 us
  local copies, waits for them, and re-layouts: 123 us -> 135 us
    ppermute x0 -> x3, waiting for transfers between devices: none -> 95.8 us  [the longest x2 77.9 us: ring_gather(): lax.ppermute(going_up, axis, [(d, (d + 1) % ways) for d in range(ways)])]
    all_gather x1 -> x0, waiting for transfers between devices: 67.8 us -> none  [on_device(): lax.all_gather(key_feat.reshape(rows, 2 * D), 'seq', axis=0, tiled=True)]
    all_gather x1, waiting for transfers between devices: 12.7 us -> 0.01 us  [on_device(): lax.all_gather(values_low, 'seq', axis=0, tiled=True)]
  transfers between devices with their start and end apart: 6 -> 8, of which waited for: 6 -> 7; matrix products, arithmetic and copies ran while one was open for 7% -> 7% of each run, Pallas kernels for 0% -> 0%
where the time goes in v1:
time: 1050 us; the launch traced here: 1040 us
  waiting for transfers between devices  524 us (50%)
  matrix products  285 us (27%)
  local copies, waits for them, and re-layouts  135 us (13%)
  other arithmetic  67.3 us (6%)
  between operations  15.9 us (2%)
    reduce_scatter x1, waiting for transfers between devices, on_device(): lax.psum_scatter(grad_mats, 'grp', scatter_dimension=0, tiled=True)  271 us
    dot_general x120, matrix products, precise(): jnp.dot(left, right, preferred_element_type=jnp.float32, precision=carefu...  170 us
    reduce_scatter x1, waiting for transfers between devices, on_device(): lax.psum_scatter(jnp.concatenate([d_keys_part.reshape(count, 2 * D), d_va...  86.2 us
    ppermute x2, waiting for transfers between devices, ring_gather(): lax.ppermute(going_up, axis, [(d, (d + 1) % ways) for d in range(ways)])  77.9 us
    psum x1, waiting for transfers between devices, on_device(): lax.psum(owned_mats.astype(jnp.bfloat16), 'seq').astype(jnp.float32)  54.8 us
    unnamed x173, local copies, waits for them, and re-layouts  26.4 us
    dynamic_update_slice x36, local copies, waits for them, and re-layouts, on_device(): lax.map(attend_back, (query_heads, key_heads, value_major, state_in, tota...  25.7 us
    dynamic_slice x48, local copies, waits for them, and re-layouts, on_device(): lax.map(attend_back, (query_heads, key_heads, value_major, state_in, tota...  23.5 us
  transfers between devices with their start and end apart: 8, of which 7 were waited for; matrix products, arithmetic and copies ran while one was open for 7% of the time, Pallas kernels for 0%

profile of v1, /device:TPU:0, one launch (start us, length us, event | category | flops | bytes accessed | tf_op | source)
XLA Modules:
  0.0 1042.9 jit_solution(13226850790410641153)
XLA Ops:
  11.6 4.2 convolution_add_fusion.3
  19.0 3.3 fusion.162
  32.5 2.9 collective-permute-start
  47.0 45.3 %collective-permute-done = bf16[512,1536]{0,1:T(8,128)(2,1)} collective-permute-done((bf16[512,1536]{0,1:T(8,128)(2,1)}, bf16[512,1536]{0,1:T(8,128)(2,1)}, u32[]{:S(2)}, u32[]{:S(2)}) %collective-permute-start) | collective-permute-done | bytes 1572896 | tf_op jit(solution)/shard_map/ppermute | solution.py:31
  96.4 2.7 copy.80
  107.3 17.9 %collective-permute-done.1 = bf16[512,1536]{0,1:T(8,128)(2,1)} collective-permute-done((bf16[512,1536]{0,1:T(8,128)(2,1)}, bf16[512,1536]{0,1:T(8,128)(2,1)}, u32[]{:S(2)}, u32[]{:S(2)}) %collective-permute-start.1) | collective-permute-done | bytes 1572896 | tf_op jit(solution)/shard_map/ppermute | solution.py:34
  126.9 32.6 %collective-permute-done.2 = bf16[512,1536]{0,1:T(8,128)(2,1)} collective-permute-done((bf16[512,1536]{0,1:T(8,128)(2,1)}, bf16[512,1536]{0,1:T(8,128)(2,1)}, u32[]{:S(2)}, u32[]{:S(2)}) %collective-permute-start.2) | collective-permute-done | bytes 1572896 | tf_op jit(solution)/shard_map/ppermute | solution.py:31
  163.8 4.7 convert_reduce_fusion
  168.4 4.6 copy.78
  173.1 5.5 fusion.171
  179.9 81.3 %while.33 = (s32[]{:T(128)}, f32[12,512,64]{1,2,0:T(8,128)}, f32[12,512]{1,0:T(8,128)}, bf16[12,512,128]{2,1,0:T(8,128)(2,1)}, bf16[12,512,128]{2,1,0:T(8,128)(2...) while((s32[]{:T(128)}, f32[12,512,64]{1,2,0:T(8,128)}, ...), condition=%wide.region_13.14_spmd.clone, body=%wide.region_11.13_spmd.clone.sunk | while | flops 194183168 | bytes 3231861 | solution.py:170
  265.9 5.0 fusion.85
  271.0 10.9 %convert_reduce_fusion.1 = (f32[3072]{0:T(1024)}, bf16[512,3072]{1,0:T(8,128)(2,1)S(1)}) fusion(f32[512,3072]{1,0:T(8,128)S(1)} %fusion.85, f32[3072]{0:T(1024)S(1)} %add.251, bf16[512,768]{1,0:T(8,128)(2,1)S(1)} %copy-done.40, bf16[768,9280]{0,1:T(8,128)(2,1)} %param.20), kind=kOutput, calls=%fused_computation.105 | convolution fusion | flops 2452091904 | bytes 14966784 | tf_op jit(solution)/shard_map/dot_general | solution.py:183
  282.0 3.5 multiply_reduce_fusion
  291.6 203.7 %while.34 = (s32[]{:T(128)}, f32[12,512,128]{1,2,0:T(8,128)}, f32[12,512,128]{1,2,0:T(8,128)}, f32[12,512,64]{1,2,0:T(8,128)}, f32[12,128,64]{1,2,0:T(8,128)}, /...) while((s32[]{:T(128)}, f32[12,512,128]{1,2,0:T(8,128)}, ...), condition=%wide.region_20.21_spmd.clone.clone, body=%wide.region_18.20_spmd.clone.clone.sunk | while | flops 723526784 | bytes 10363109 | solution.py:215
  495.3 5.1 multiply_convert_fusion.1
  500.5 5.4 multiply_convert_fusion
  505.8 11.6 %pad_maximum_fusion = bf16[2048,2304]{0,1:T(8,128)(2,1)} fusion(bf16[2048,768]{0,1:T(8,128)(2,1)S(1)} %bitcast.307, bf16[2048,1536]{0,1:T(8,128)(2,1)S(1)} %bitcast.302), kind=kLoop, calls=%fused_computation.92 | loop fusion | flops 18874368 | bytes 18874368 | tf_op jit(solution)/shard_map/concatenate | solution.py:232
  518.9 3.4 multiply_reduce_fusion.4
  525.6 86.2 %reduce-scatter.6.cloned.1.call-done = bf16[512,2304]{0,1:T(8,128)(2,1)} async-done(((bf16[2048,2304]{0,1:T(8,128)(2,1)}), bf16[512,2304]{0,1:T(8,128)(2,1)}) %reduce-scatter.6.cloned.1.call-update) | async-done | bytes 2359312 | tf_op jit(solution)/shard_map/reduce_scatter | solution.py:231
  625.4 5.4 convolution_dynamic-update-slice_fusion
  633.1 5.5 convolution_dynamic-update-slice_fusion.1
  638.7 5.5 bitcast_dynamic-update-slice_fusion
  647.6 6.0 fusion.110
  655.0 270.6 %reduce-scatter.8.cloned.1.call-done = f32[96,9280]{1,0:T(8,128)} async-done(((f32[768,9280]{1,0:T(8,128)}), f32[96,9280]{1,0:T(8,128)}) %reduce-scatter.8.cloned.1.call-update) | async-done | bytes 3563536 | tf_op jit(solution)/shard_map/reduce_scatter | solution.py:268
  925.6 3.4 convert_element_type.146
  929.8 9.6 add_convert_fusion
  940.9 16.5 %reduce-scatter.10.cloned.1.call-done = f32[96,13]{1,0:T(8,128)} async-done(((f32[768,13]{1,0:T(8,128)}), f32[96,13]{1,0:T(8,128)}) %reduce-scatter.10.cloned.1.call-update) | async-done | bytes 5008
  958.3 9.9 psum.15
  969.4 54.8 %all-reduce.2.cloned.1.call-done = bf16[96,9280]{1,0:T(8,128)(2,1)} async-done(((bf16[96,9280]{1,0:T(8,128)(2,1)}), bf16[96,9280]{1,0:T(8,128)(2,1)}) %all-reduce.2.cloned.1.call-update) | async-done | bytes 1781776 | tf_op jit(solution)/shard_map/psum | solution.py:272
  1024.2 8.9 fusion.158
  1033.1 2.8 multiply_add_fusion.1
  (585 shorter events, 372.2 us)
Async XLA Ops:
  7.2 161.2 %all-gather.2.cloned.1.call-start = ((), (), s32[]{:S(2)}) async-start(), calls=%async_computation.3 | async-start | bytes 3932160 | tf_op jit(solution)/shard_map/all_gather | solution.py:144
  8.7 7.1 copy-start.53
  8.7 7.1 copy-start.71
  8.7 257.2 %copy-start.69 = (f32[768]{0:T(1024)}, f32[768]{0:T(1024)S(1)}, u32[]{:S(2)}) copy-start(f32[768]{0:T(1024)S(1)} %get-tuple-element.327) | copy-start | bytes 9220
  8.7 276.8 %copy-start.51 = (f32[768]{0:T(1024)}, f32[768]{0:T(1024)S(1)}, u32[]{:S(2)}) copy-start(f32[768]{0:T(1024)S(1)} %get-tuple-element.325) | copy-start | bytes 9220
  18.9 592.8 %reduce-scatter.6.cloned.1.call-start = ((), (), s32[]{:S(2)}) async-start(), calls=%async_computation.4 | async-start | bytes 11796480 | tf_op jit(solution)/shard_map/reduce_scatter | solution.py:231
  22.4 17.7 %copy-start.30 = (bf16[768,64]{1,0:T(8,128)(2,1)}, bf16[768,64]{1,0:T(8,128)(2,1)S(1)}, u32[]{:S(2)}) copy-start(bf16[768,64]{1,0:T(8,128)(2,1)S(1)} %copy.136) | copy-start | bytes 294916
  30.8 6.3 copy-start.19
  32.5 59.9 %collective-permute-start = (bf16[512,1536]{0,1:T(8,128)(2,1)}, bf16[512,1536]{0,1:T(8,128)(2,1)}, u32[]{:S(2)}, u32[]{:S(2)}) collective-permute-start(bf16[512,1536]{0,1:T(8,128)(2,1)} %bitcast.9), channel_id=1, source_target_pairs={{0,8},{8,16},{16,24},{24,0},{1,9},{9,17},{17,25},{25,1},{2,10},{10... | collective-permute-start | bytes 4718600 | tf_op jit(solution)/shard_map/ppermute | solution.py:31
  35.4 89.8 %collective-permute-start.1 = (bf16[512,1536]{0,1:T(8,128)(2,1)}, bf16[512,1536]{0,1:T(8,128)(2,1)}, u32[]{:S(2)}, u32[]{:S(2)}) collective-permute-start(bf16[512,1536]{0,1:T(8,128)(2,1)} %bitcast.9), channel_id=1, source_target_pairs={{0,24},{8,0},{16,8},{24,16},{1,25},{9,1},{17,9},{25,17},{2,26},{10... | collective-permute-start | bytes 4718600 | tf_op jit(solution)/shard_map/ppermute | solution.py:34
  92.3 67.1 %collective-permute-start.2 = (bf16[512,1536]{0,1:T(8,128)(2,1)}, bf16[512,1536]{0,1:T(8,128)(2,1)}, u32[]{:S(2)}, u32[]{:S(2)}) collective-permute-start(bf16[512,1536]{0,1:T(8,128)(2,1)} %collective-permute-done), channel_id=1, source_target_pairs={{0,8},{8,16},{16,24},{24,0},{1,9},{9,17},{17,25},{25,1},{2,10},{10... | collective-permute-start | bytes 4718600 | tf_op jit(solution)/shard_map/ppermute | solution.py:31
  92.5 178.4 %copy-start.55 = (f32[3072]{0:T(1024)}, f32[3072]{0:T(1024)S(1)}, u32[]{:S(2)}) copy-start(f32[3072]{0:T(1024)S(1)} %add.251) | copy-start | bytes 36868
  265.5 20.0 %copy-start.27 = (f32[512,768]{1,0:T(8,128)}, f32[512,768]{1,0:T(8,128)S(1)}, u32[]{:S(2)}) copy-start(f32[512,768]{1,0:T(8,128)S(1)} %get-tuple-element.409) | copy-start | bytes 4718596
  265.6 19.9 %copy-start.47 = (f32[512]{0:T(512)}, f32[512]{0:T(512)S(1)}, u32[]{:S(2)}) copy-start(f32[512]{0:T(512)S(1)} %broadcast_multiply_fusion.5) | copy-start | bytes 6148
  265.9 19.6 %copy-start.60 = (f32[512]{0:T(512)}, f32[512]{0:T(512)S(1)}, u32[]{:S(2)}) copy-start(f32[512]{0:T(512)S(1)} %add_rsqrt_fusion) | copy-start | bytes 6148
  265.9 16.0 %slice-start = ((s8[14254080]{0:T(1024)(128)(4,1)}), s8[4194304]{0:T(1024)(128)(4,1)S(1)}, s32[]{:S(2)}) async-start(s8[14254080]{0:T(1024)(128)(4,1)} %bitcast.337), calls=%async_computation.8 | async-start | bytes 8388608
  265.9 16.0 %slice-start.1 = ((s8[14254080]{0:T(1024)(128)(4,1)}), s8[4194304]{0:T(1024)(128)(4,1)S(1)}, s32[]{:S(2)}) async-start(s8[14254080]{0:T(1024)(128)(4,1)} %bitcast.337), calls=%async_computation.9 | async-start | bytes 8388608
  271.0 11.0 %copy-start.78 = (f32[512,3072]{1,0:T(8,128)}, f32[512,3072]{1,0:T(8,128)S(1)}, u32[]{:S(2)}) copy-start(f32[512,3072]{1,0:T(8,128)S(1)} %fusion.85) | copy-start | bytes 18874372
  271.0 11.0 %slice-start.2 = ((s8[14254080]{0:T(1024)(128)(4,1)}), s8[4194304]{0:T(1024)(128)(4,1)S(1)}, s32[]{:S(2)}) async-start(s8[14254080]{0:T(1024)(128)(4,1)} %bitcast.337), calls=%async_computation.10 | async-start | bytes 8388608
  271.0 11.0 %slice-start.3 = ((s8[14254080]{0:T(1024)(128)(4,1)}), s8[1671168]{0:T(1024)(128)(4,1)S(1)}, s32[]{:S(2)}) async-start(s8[14254080]{0:T(1024)(128)(4,1)} %bitcast.337), calls=%async_computation.11 | async-start | bytes 3342336
  517.5 408.2 %reduce-scatter.8.cloned.1.call-start = ((), (), s32[]{:S(2)}) async-start(), calls=%async_computation.5 | async-start | bytes 32292864 | tf_op jit(solution)/shard_map/reduce_scatter | solution.py:268
  625.4 7.7 copy-start.77
  630.8 7.8 slice-start.5
  645.0 312.4 %reduce-scatter.10.cloned.1.call-start = ((), (), s32[]{:S(2)}) async-start(), calls=%async_computation.7 | async-start | bytes 442368
  654.7 369.5 %all-reduce.2.cloned.1.call-start = ((), (), s32[]{:S(2)}) async-start(), calls=%async_computation.6 | async-start | bytes 3588096 | tf_op jit(solution)/shard_map/psum | solution.py:272
  929.8 9.6 copy-start.39
  939.4 28.7 %copy-start.63 = (f32[96,13]{0,1:T(8,128)S(1)}, f32[96,13]{0,1:T(8,128)}, u32[]{:S(2)}) copy-start(f32[96,13]{0,1:T(8,128)} %param.23) | copy-start | bytes 14980
  939.4 28.7 %copy-start.64 = (f32[96,13]{0,1:T(8,128)S(1)}, f32[96,13]{0,1:T(8,128)}, u32[]{:S(2)}) copy-start(f32[96,13]{0,1:T(8,128)} %param.27) | copy-start | bytes 14980
  939.4 28.7 %copy-start.65 = (f32[96,13]{0,1:T(8,128)S(1)}, f32[96,13]{0,1:T(8,128)}, u32[]{:S(2)}) copy-start(f32[96,13]{0,1:T(8,128)} %param.25) | copy-start | bytes 14980
  939.4 29.4 %copy-start.62 = (f32[96,13]{0,1:T(8,128)S(1)}, f32[96,13]{0,1:T(8,128)}, u32[]{:S(2)}) copy-start(f32[96,13]{0,1:T(8,128)} %param.29) | copy-start | bytes 14980
  968.8 64.3 %copy-start.44 = (f32[96,13]{0,1:T(8,128)}, f32[96,13]{0,1:T(8,128)S(1)}, u32[]{:S(2)}) copy-start(f32[96,13]{0,1:T(8,128)S(1)} %get-tuple-element.378) | copy-start | bytes 14980
  1024.2 8.9 copy-start.32
  (73 other events, 185.7 us)
Sparse Core Ops, SparseCore 0:
  19.0 67.7 all-gather.1
  517.6 94.1 reduce-scatter.5
  645.2 280.4 reduce-scatter.7
  928.3 29.0 reduce-scatter.9
  961.4 62.7 all-reduce.1
